TPU v7x, 32 devices: a whole 2x2x4 slice. The times are simulated.
32 devices in a mesh: seqhi: 8 (over y, x, core), seqlo: 4 (over z).
Axes of the slice: x: 2, y: 2, z: 4, core: 2. Of those that a mesh axis runs over, the one named last changes fastest.
Arguments:
- tokens: bfloat16 [32768, 768], P(('seqhi', 'seqlo')), may hold values from -6 to 6
- cotangent: bfloat16 [32768, 768], P(('seqhi', 'seqlo')), may hold values from -6 to 6
- first_kernel_weight: bfloat16 [2304, 384], replicated, may hold values from -0.125 to 0.125
- first_pointwise_weight: bfloat16 [768, 384], replicated, may hold values from -0.3125 to 0.3125
- second_kernel_weight: bfloat16 [2304, 384], replicated, may hold values from -0.125 to 0.125
- second_pointwise_weight: bfloat16 [768, 384], replicated, may hold values from -0.3125 to 0.3125
Outputs:
- output: bfloat16 [32768, 768], P(('seqhi', 'seqlo'))
- token_rows_gradient: bfloat16 [32768, 768], P(('seqhi', 'seqlo'))
- first_kernel_gradient: float32 [2304, 384], P(('seqhi', 'seqlo'))
- first_pointwise_gradient: float32 [768, 384], P(('seqhi', 'seqlo'))
- second_kernel_gradient: float32 [2304, 384], P(('seqhi', 'seqlo'))
- second_pointwise_gradient: float32 [768, 384], P(('seqhi', 'seqlo'))
All inputs are finite; a program needn't handle non-finite values.
Results may differ from a plain program's by a relative error of at most 0.015.
Values may be sent and summed in bfloat16 or wider, within the bound.
A program may use at most 128 MiB of HBM per device.

v0:
```python
import jax
import jax.numpy as jnp
from jax import lax
from jax.sharding import PartitionSpec as P

FIRST_SPACING = 4096
SECOND_SPACING = 8192


def shifted(x, axis, by):
    devices = lax.axis_size(axis)
    pairs = [(i, i + by) for i in range(devices) if 0 <= i + by < devices]
    return lax.ppermute(x, axis, pairs)


def contract_rows(left, right):
    return lax.dot_general(
        left, right, (((0,), (0,)), ((), ())), preferred_element_type=jnp.float32
    )


def tap_inputs(tokens, device_reach):
    earlier = shifted(tokens, ("seqhi", "seqlo"), device_reach)
    later = shifted(tokens, ("seqhi", "seqlo"), -device_reach)
    return (earlier, tokens, later)


def residual_block_forward(tokens, conv_weight, proj_weight, device_reach):
    width = tokens.shape[1]
    tap_rows = tap_inputs(tokens, device_reach)
    pre = jnp.dot(tokens, conv_weight[width : 2 * width], preferred_element_type=jnp.float32)
    pre = pre + jnp.dot(tap_rows[0], conv_weight[0:width], preferred_element_type=jnp.float32)
    pre = pre + jnp.dot(
        tap_rows[2], conv_weight[2 * width : 3 * width], preferred_element_type=jnp.float32
    )
    inner = jax.nn.gelu(pre).astype(jnp.bfloat16)
    mixed = lax.dot_general(
        inner, proj_weight, (((1,), (1,)), ((), ())), preferred_element_type=jnp.float32
    )
    result = (tokens.astype(jnp.float32) + mixed).astype(jnp.bfloat16)
    return (result, tap_rows, pre, inner)


def reduce_terms(grad_terms):
    outer_count = lax.axis_size("seqhi")
    inner_count = lax.axis_size("seqlo")
    reordered = []
    for member in grad_terms:
        total_rows = member.shape[0]
        blocked = member.reshape(
            outer_count, inner_count, total_rows // (outer_count * inner_count), member.shape[1]
        )
        reordered.append(jnp.transpose(blocked, (1, 0, 2, 3)).reshape(total_rows, member.shape[1]))
    partial_sums = (
        lax.psum_scatter(
            reordered[0].astype(jnp.bfloat16), "seqlo", scatter_dimension=0, tiled=True
        ).astype(jnp.float32),
        lax.psum_scatter(
            reordered[1].astype(jnp.bfloat16), "seqlo", scatter_dimension=0, tiled=True
        ).astype(jnp.float32),
    )
    return (
        lax.psum_scatter(
            partial_sums[0].astype(jnp.bfloat16), "seqhi", scatter_dimension=0, tiled=True
        ).astype(jnp.float32),
        lax.psum_scatter(
            partial_sums[1].astype(jnp.bfloat16), "seqhi", scatter_dimension=0, tiled=True
        ).astype(jnp.float32),
    )


def residual_block_backward(grad_out, tap_rows, pre, inner, conv_weight, proj_weight, device_reach):
    width = grad_out.shape[1]
    grad_proj_term = contract_rows(grad_out, inner)
    grad_inner = jnp.dot(grad_out, proj_weight, preferred_element_type=jnp.float32)
    _, pullback = jax.vjp(jax.nn.gelu, pre)
    grad_pre = pullback(grad_inner)[0].astype(jnp.bfloat16)
    later = shifted(grad_pre, ("seqhi", "seqlo"), -device_reach)
    earlier = shifted(grad_pre, ("seqhi", "seqlo"), device_reach)
    grad_conv_term = jnp.concatenate(
        [contract_rows(tap_rows[tap_index], grad_pre) for tap_index in range(3)], 0
    )
    grad_in = grad_out.astype(jnp.float32)
    moved = (later, grad_pre, earlier)
    for tap_index in range(3):
        grad_in = grad_in + lax.dot_general(
            moved[tap_index],
            conv_weight[tap_index * width : (tap_index + 1) * width],
            (((1,), (1,)), ((), ())),
            preferred_element_type=jnp.float32,
        )
    grad_conv, grad_proj = reduce_terms((grad_conv_term, grad_proj_term))
    return (grad_in.astype(jnp.bfloat16), grad_conv, grad_proj)


def per_device(
    tokens,
    cotangent,
    first_kernel_weight,
    first_pointwise_weight,
    second_kernel_weight,
    second_pointwise_weight,
):
    shard_row_block = tokens.shape[0]
    first_halo_span = FIRST_SPACING // shard_row_block
    second_halo_span = SECOND_SPACING // shard_row_block
    between_blocks_state, rows_first, first_preactivation, first_hidden_state = (
        residual_block_forward(tokens, first_kernel_weight, first_pointwise_weight, first_halo_span)
    )
    output, rows_second, second_preactivation, second_hidden_state = residual_block_forward(
        between_blocks_state, second_kernel_weight, second_pointwise_weight, second_halo_span
    )
    between_blocks_gradient, second_kernel_gradient, second_pointwise_gradient = (
        residual_block_backward(
            cotangent,
            rows_second,
            second_preactivation,
            second_hidden_state,
            second_kernel_weight,
            second_pointwise_weight,
            second_halo_span,
        )
    )
    token_rows_gradient, first_kernel_gradient, first_pointwise_gradient = residual_block_backward(
        between_blocks_gradient,
        rows_first,
        first_preactivation,
        first_hidden_state,
        first_kernel_weight,
        first_pointwise_weight,
        first_halo_span,
    )
    return (
        output,
        token_rows_gradient,
        first_kernel_gradient,
        first_pointwise_gradient,
        second_kernel_gradient,
        second_pointwise_gradient,
    )


def solution(mesh):
    placed = (P(("seqhi", "seqlo"), None), P(("seqhi", "seqlo"), None), P(), P(), P(), P())
    return jax.shard_map(
        per_device,
        mesh=mesh,
        in_specs=placed,
        out_specs=(
            P(("seqhi", "seqlo"), None),
            P(("seqhi", "seqlo"), None),
            P(("seqhi", "seqlo"), None),
            P(("seqhi", "seqlo"), None),
            P(("seqhi", "seqlo"), None),
            P(("seqhi", "seqlo"), None),
        ),
        check_vma=False,
    )
```

profile of v0, /device:TPU:0, one launch (start us, length us, event | category | flops | bytes accessed | tf_op | source)
XLA Modules:
  0.0 421.7 jit_solution(11298964360908124664)
XLA Ops:
  7.2 2.6 collective-permute-start
  9.9 1.3 collective-permute-start.1
  11.2 2.5 fusion.36
  13.7 1.0 fusion.32
  14.7 0.2 copy-done.9
  14.9 2.5 collective-permute-done.1
  17.4 1.0 add_add_fusion.1
  18.4 1.1 copy-done.11
  19.6 1.3 add_convert_fusion.3
  20.9 33.1 %collective-permute-start.2 = (bf16[1024,768]{1,0:T(8,128)(2,1)S(1)}, bf16[1024,768]{1,0:T(8,128)(2,1)S(1)}, u32[]{:S(2)}, u32[]{:S(2)}) collective-permute-start(bf16[1024,768]{1,0:T(8,128)(2,1)S(1)} %add_convert_fusion.3), channel_id=1, source_target_pairs={{0,8},{1,9},{2,10},{3,11},{4,12},{5,13},{6,14},{7,15},{8,16},{9,17... | collective-permute-start | bytes 4718600 | tf_op jit(solution)/shard_map/ppermute | solution.py:13
  54.0 1.3 collective-permute-start.3
  55.3 1.0 fusion.38
  56.3 1.0 fusion.26
  57.3 30.7 %collective-permute-done.2 = bf16[1024,768]{1,0:T(8,128)(2,1)S(1)} collective-permute-done((bf16[1024,768]{1,0:T(8,128)(2,1)S(1)}, bf16[1024,768]{1,0:T(8,128)(2,1)S(1)}, u32[]{:S(2)}, u32[]{:S(2)}) %collective-permute-start.2) | collective-permute-done | bytes 1572896 | tf_op jit(solution)/shard_map/ppermute | solution.py:13
  88.0 1.0 fusion.22
  89.0 0.2 copy-done.17
  89.2 34.6 %collective-permute-done.3 = bf16[1024,768]{1,0:T(8,128)(2,1)S(1)} collective-permute-done((bf16[1024,768]{1,0:T(8,128)(2,1)S(1)}, bf16[1024,768]{1,0:T(8,128)(2,1)S(1)}, u32[]{:S(2)}, u32[]{:S(2)}) %collective-permute-start.3) | collective-permute-done | bytes 1572896 | tf_op jit(solution)/shard_map/ppermute | solution.py:13
  123.8 2.8 fusion.13
  126.7 1.3 collective-permute-start.4
  127.9 5.5 %collective-permute-start.5 = (bf16[1024,384]{1,0:T(8,128)(2,1)}, bf16[1024,384]{1,0:T(8,128)(2,1)}, u32[]{:S(2)}, u32[]{:S(2)}) collective-permute-start(bf16[1024,384]{1,0:T(8,128)(2,1)} %get-tuple-element.6), channel_id=1, source_target_pairs={{0,8},{1,9},{2,10},{3,11},{4,12},{5,13},{6,14},{7,15},{8,16},{9,17... | collective-permute-start | bytes 2359304 | tf_op jit(solution)/shard_map/ppermute | solution.py:13
  133.5 1.0 fusion.17
  134.5 0.3 copy.30
  134.8 0.9 copy.31
  135.7 0.2 reduce-scatter.19.cloned.1.call-start
  135.9 2.4 fusion.24
  138.4 10.9 %collective-permute-done.4 = bf16[1024,384]{1,0:T(8,128)(2,1)} collective-permute-done((bf16[1024,384]{1,0:T(8,128)(2,1)}, bf16[1024,384]{1,0:T(8,128)(2,1)}, u32[]{:S(2)}, u32[]{:S(2)}) %collective-permute-start.4) | collective-permute-done | bytes 786464 | tf_op jit(solution)/shard_map/ppermute | solution.py:13
  149.3 2.1 fusion.20
  151.4 2.4 add_convert_fusion.1
  153.8 1.2 copy-done.2
  155.0 1.1 convolution_convert_fusion.4
  156.1 0.9 copy.28
  157.1 0.0 reduce-scatter.21.cloned.1.call-start
  157.1 2.7 convolution_convert_fusion.2
  159.9 2.3 convolution_convert_fusion.1
  162.1 2.1 convolution_convert_fusion.3
  164.3 0.2 pad_maximum_fusion.1
  164.5 1.4 copy.29
  165.9 0.0 reduce-scatter.31.cloned.1.call-start
  166.0 3.7 fusion.6
  169.7 1.6 fusion.15
  171.4 1.6 fusion.16
  173.0 1.7 fusion.14
  174.7 1.5 pad_maximum_fusion
  176.2 2.3 copy.26
  178.5 2.9 copy.27
  181.5 11.2 %reduce-scatter.19.cloned.1.call-done = bf16[192,384]{1,0:T(8,128)(2,1)} async-done(((bf16[768,384]{1,0:T(8,128)(2,1)}), bf16[192,384]{1,0:T(8,128)(2,1)}) %reduce-scatter.19.cloned.1.call-update) | async-done | bytes 147472 | tf_op jit(solution)/shard_map/reduce_scatter | solution.py:58
  192.7 1.3 collective-permute-start.6
  194.0 4.0 collective-permute-start.7
  198.0 33.9 %reduce-scatter.21.cloned.1.call-done = bf16[576,384]{1,0:T(8,128)(2,1)} async-done(((bf16[2304,384]{1,0:T(8,128)(2,1)}), bf16[576,384]{1,0:T(8,128)(2,1)}) %reduce-scatter.21.cloned.1.call-update) | async-done | bytes 442384 | tf_op jit(solution)/shard_map/reduce_scatter | solution.py:55
  231.9 0.3 reduce-scatter.25.cloned.1.call-start
  232.2 3.8 add_convert_fusion.2
  236.0 3.7 fusion.34
  239.7 26.5 %reduce-scatter.31.cloned.1.call-done = bf16[24,384]{1,0:T(8,128)(2,1)} async-done(((bf16[192,384]{1,0:T(8,128)(2,1)}), bf16[24,384]{1,0:T(8,128)(2,1)}) %reduce-scatter.31.cloned.1.call-update) | async-done | bytes 18448
  266.2 1.3 convert_element_type.133
  267.5 39.3 %reduce-scatter.17.cloned.1.call-done = bf16[576,384]{1,0:T(8,128)(2,1)} async-done(((bf16[2304,384]{1,0:T(8,128)(2,1)}), bf16[576,384]{1,0:T(8,128)(2,1)}) %reduce-scatter.17.cloned.1.call-update) | async-done | bytes 442384 | tf_op jit(solution)/shard_map/reduce_scatter | solution.py:55
  306.9 2.4 fusion.30
  309.4 0.3 copy-done.1
  309.6 3.6 add_convert_fusion
  313.2 27.9 %reduce-scatter.27.cloned.1.call-done = bf16[24,384]{1,0:T(8,128)(2,1)} async-done(((bf16[192,384]{1,0:T(8,128)(2,1)}), bf16[24,384]{1,0:T(8,128)(2,1)}) %reduce-scatter.27.cloned.1.call-update) | async-done | bytes 18448
  341.2 1.3 convert_element_type.123
  342.5 34.7 %reduce-scatter.29.cloned.1.call-done = bf16[72,384]{1,0:T(8,128)(2,1)} async-done(((bf16[576,384]{1,0:T(8,128)(2,1)}), bf16[72,384]{1,0:T(8,128)(2,1)}) %reduce-scatter.29.cloned.1.call-update) | async-done | bytes 55312
  377.3 1.5 convert_element_type.127
  378.7 34.6 %reduce-scatter.25.cloned.1.call-done = bf16[72,384]{1,0:T(8,128)(2,1)} async-done(((bf16[576,384]{1,0:T(8,128)(2,1)}), bf16[72,384]{1,0:T(8,128)(2,1)}) %reduce-scatter.25.cloned.1.call-update) | async-done | bytes 55312
  413.3 1.5 convert_element_type.118
  (60 shorter events, 0.4 us)
Async XLA Ops:
  7.2 12.4 %copy-start = (bf16[768,384]{1,0:T(8,128)(2,1)S(1)}, bf16[768,384]{1,0:T(8,128)(2,1)}, u32[]{:S(2)}) copy-start(bf16[768,384]{1,0:T(8,128)(2,1)} %param.9) | copy-start | bytes 1769476
  7.2 167.5 %reduce-scatter.23.cloned.1.call-start = ((), (), s32[]{:S(2)}) async-start(), calls=%async_computation.11 | async-start | bytes 737280 | tf_op jit(solution)/shard_map/reduce_scatter | solution.py:58
  7.2 6.5 %copy-start.4 = (bf16[2304,384]{1,0:T(8,128)(2,1)S(1)}, bf16[2304,384]{1,0:T(8,128)(2,1)}, u32[]{:S(2)}) copy-start(bf16[2304,384]{1,0:T(8,128)(2,1)} %param.8) | copy-start | bytes 5308420
  7.2 6.5 %collective-permute-start = (bf16[1024,768]{1,0:T(8,128)(2,1)}, bf16[1024,768]{1,0:T(8,128)(2,1)S(1)}, u32[]{:S(2)}, u32[]{:S(2)}) collective-permute-start(bf16[1024,768]{1,0:T(8,128)(2,1)} %param.6), channel_id=1, source_target_pairs={{0,4},{1,5},{2,6},{3,7},{4,8},{5,9},{6,10},{7,11},{8,12},{9,13},{1... | collective-permute-start | bytes 4718600 | tf_op jit(solution)/shard_map/ppermute | solution.py:13
  9.9 7.5 %collective-permute-start.1 = (bf16[1024,768]{1,0:T(8,128)(2,1)}, bf16[1024,768]{1,0:T(8,128)(2,1)S(1)}, u32[]{:S(2)}, u32[]{:S(2)}) collective-permute-start(bf16[1024,768]{1,0:T(8,128)(2,1)} %param.6), channel_id=1, source_target_pairs={{4,0},{5,1},{6,2},{7,3},{8,4},{9,5},{10,6},{11,7},{12,8},{13,9},{1... | collective-permute-start | bytes 4718600 | tf_op jit(solution)/shard_map/ppermute | solution.py:13
  13.7 1.2 copy-start.9
  14.9 4.7 %copy-start.7 = (bf16[1024,768]{1,0:T(8,128)(2,1)S(1)}, bf16[1024,768]{1,0:T(8,128)(2,1)}, u32[]{:S(2)}) copy-start(bf16[1024,768]{1,0:T(8,128)(2,1)} %param.6) | copy-start | bytes 4718596
  18.4 1.1 copy-start.11
  19.6 35.8 %copy-start.13 = (bf16[1024,768]{1,0:T(8,128)(2,1)S(1)}, bf16[1024,768]{1,0:T(8,128)(2,1)}, u32[]{:S(2)}) copy-start(bf16[1024,768]{1,0:T(8,128)(2,1)} %param.7) | copy-start | bytes 4718596
  19.6 35.8 %copy-start.21 = (bf16[768,384]{1,0:T(8,128)(2,1)S(1)}, bf16[768,384]{1,0:T(8,128)(2,1)}, u32[]{:S(2)}) copy-start(bf16[768,384]{1,0:T(8,128)(2,1)} %param.11) | copy-start | bytes 1769476
  20.8 35.5 %copy-start.15 = (bf16[1024,768]{1,0:T(8,128)(2,1)}, bf16[1024,768]{1,0:T(8,128)(2,1)S(1)}, u32[]{:S(2)}) copy-start(bf16[1024,768]{1,0:T(8,128)(2,1)S(1)} %add_convert_fusion.3) | copy-start | bytes 4718596
  20.9 35.5 %copy-start.5 = (bf16[2304,384]{1,0:T(8,128)(2,1)S(1)}, bf16[2304,384]{1,0:T(8,128)(2,1)}, u32[]{:S(2)}) copy-start(bf16[2304,384]{1,0:T(8,128)(2,1)} %param.10) | copy-start | bytes 5308420
  20.9 67.1 %collective-permute-start.2 = (bf16[1024,768]{1,0:T(8,128)(2,1)S(1)}, bf16[1024,768]{1,0:T(8,128)(2,1)S(1)}, u32[]{:S(2)}, u32[]{:S(2)}) collective-permute-start(bf16[1024,768]{1,0:T(8,128)(2,1)S(1)} %add_convert_fusion.3), channel_id=1, source_target_pairs={{0,8},{1,9},{2,10},{3,11},{4,12},{5,13},{6,14},{7,15},{8,16},{9,17... | collective-permute-start | bytes 4718600 | tf_op jit(solution)/shard_map/ppermute | solution.py:13
  54.0 69.8 %collective-permute-start.3 = (bf16[1024,768]{1,0:T(8,128)(2,1)S(1)}, bf16[1024,768]{1,0:T(8,128)(2,1)S(1)}, u32[]{:S(2)}, u32[]{:S(2)}) collective-permute-start(bf16[1024,768]{1,0:T(8,128)(2,1)S(1)} %add_convert_fusion.3), channel_id=1, source_target_pairs={{8,0},{9,1},{10,2},{11,3},{12,4},{13,5},{14,6},{15,7},{16,8},{17,9... | collective-permute-start | bytes 4718600 | tf_op jit(solution)/shard_map/ppermute | solution.py:13
  88.0 1.2 copy-start.17
  123.8 2.8 copy-start.19
  126.7 6.8 %copy-start.23 = (f32[1024,384]{1,0:T(8,128)}, f32[1024,384]{1,0:T(8,128)S(1)}, u32[]{:S(2)}) copy-start(f32[1024,384]{1,0:T(8,128)S(1)} %get-tuple-element.7) | copy-start | bytes 4718596
  126.7 22.6 %collective-permute-start.4 = (bf16[1024,384]{1,0:T(8,128)(2,1)}, bf16[1024,384]{1,0:T(8,128)(2,1)}, u32[]{:S(2)}, u32[]{:S(2)}) collective-permute-start(bf16[1024,384]{1,0:T(8,128)(2,1)} %get-tuple-element.6), channel_id=1, source_target_pairs={{8,0},{9,1},{10,2},{11,3},{12,4},{13,5},{14,6},{15,7},{16,8},{17,9... | collective-permute-start | bytes 2359304 | tf_op jit(solution)/shard_map/ppermute | solution.py:13
  127.9 23.5 %collective-permute-start.5 = (bf16[1024,384]{1,0:T(8,128)(2,1)}, bf16[1024,384]{1,0:T(8,128)(2,1)}, u32[]{:S(2)}, u32[]{:S(2)}) collective-permute-start(bf16[1024,384]{1,0:T(8,128)(2,1)} %get-tuple-element.6), channel_id=1, source_target_pairs={{0,8},{1,9},{2,10},{3,11},{4,12},{5,13},{6,14},{7,15},{8,16},{9,17... | collective-permute-start | bytes 2359304 | tf_op jit(solution)/shard_map/ppermute | solution.py:13
  135.7 57.0 %reduce-scatter.19.cloned.1.call-start = ((), (), s32[]{:S(2)}) async-start(), calls=%async_computation.9 | async-start | bytes 737280 | tf_op jit(solution)/shard_map/reduce_scatter | solution.py:58
  135.9 13.4 %copy-start.6 = (bf16[2304,384]{1,0:T(8,128)(2,1)S(1)}, bf16[2304,384]{1,0:T(8,128)(2,1)}, u32[]{:S(2)}) copy-start(bf16[2304,384]{1,0:T(8,128)(2,1)} %param.10) | copy-start | bytes 5308420
  138.3 13.1 %copy-start.14 = (bf16[1024,768]{1,0:T(8,128)(2,1)S(1)}, bf16[1024,768]{1,0:T(8,128)(2,1)}, u32[]{:S(2)}) copy-start(bf16[1024,768]{1,0:T(8,128)(2,1)} %param.7) | copy-start | bytes 4718596
  151.4 3.6 copy-start.12
  153.8 1.2 copy-start.2
  157.1 74.8 %reduce-scatter.21.cloned.1.call-start = ((), (), s32[]{:S(2)}) async-start(), calls=%async_computation.10 | async-start | bytes 2211840 | tf_op jit(solution)/shard_map/reduce_scatter | solution.py:55
  157.1 2.7 copy-start.20
  159.9 2.3 copy-start.18
  165.9 100.3 %reduce-scatter.31.cloned.1.call-start = ((), (), s32[]{:S(2)}) async-start(), calls=%async_computation.15 | async-start | bytes 165888
  165.9 3.7 copy-start.8
  171.3 1.6 copy-start.10
  174.7 132.2 %reduce-scatter.17.cloned.1.call-start = ((), (), s32[]{:S(2)}) async-start(), calls=%async_computation.8 | async-start | bytes 2211840 | tf_op jit(solution)/shard_map/reduce_scatter | solution.py:55
  181.4 50.8 %copy-start.16 = (bf16[1024,768]{1,0:T(8,128)(2,1)S(1)}, bf16[1024,768]{1,0:T(8,128)(2,1)}, u32[]{:S(2)}) copy-start(bf16[1024,768]{1,0:T(8,128)(2,1)} %copy-done.15) | copy-start | bytes 4718596
  181.4 50.8 %copy-start.22 = (bf16[768,384]{1,0:T(8,128)(2,1)S(1)}, bf16[768,384]{1,0:T(8,128)(2,1)}, u32[]{:S(2)}) copy-start(bf16[768,384]{1,0:T(8,128)(2,1)} %param.11) | copy-start | bytes 1769476
  181.4 159.8 %reduce-scatter.27.cloned.1.call-start = ((), (), s32[]{:S(2)}) async-start(), calls=%async_computation.13 | async-start | bytes 165888
  192.7 184.6 %reduce-scatter.29.cloned.1.call-start = ((), (), s32[]{:S(2)}) async-start(), calls=%async_computation.14 | async-start | bytes 497664
  192.7 114.2 %collective-permute-start.6 = (bf16[1024,384]{1,0:T(8,128)(2,1)S(1)}, bf16[1024,384]{1,0:T(8,128)(2,1)}, u32[]{:S(2)}, u32[]{:S(2)}) collective-permute-start(bf16[1024,384]{1,0:T(8,128)(2,1)S(1)} %fusion.6), channel_id=1, source_target_pairs={{4,0},{5,1},{6,2},{7,3},{8,4},{9,5},{10,6},{11,7},{12,8},{13,9},{1... | collective-permute-start | bytes 2359304 | tf_op jit(solution)/shard_map/ppermute | solution.py:13
  194.0 115.4 %collective-permute-start.7 = (bf16[1024,384]{1,0:T(8,128)(2,1)S(1)}, bf16[1024,384]{1,0:T(8,128)(2,1)}, u32[]{:S(2)}, u32[]{:S(2)}) collective-permute-start(bf16[1024,384]{1,0:T(8,128)(2,1)S(1)} %fusion.6), channel_id=1, source_target_pairs={{0,4},{1,5},{2,6},{3,7},{4,8},{5,9},{6,10},{7,11},{8,12},{9,13},{1... | collective-permute-start | bytes 2359304 | tf_op jit(solution)/shard_map/ppermute | solution.py:13
  231.9 181.5 %reduce-scatter.25.cloned.1.call-start = ((), (), s32[]{:S(2)}) async-start(), calls=%async_computation.12 | async-start | bytes 497664
  306.8 2.5 copy-start.3
  306.9 2.8 copy-start.1
Sparse Core Ops, SparseCore 0:
  135.8 21.5 reduce-scatter.22
  159.6 32.9 reduce-scatter.18
  195.0 36.8 reduce-scatter.20
  234.8 31.3 reduce-scatter.30
  268.3 38.4 reduce-scatter.16
  309.7 31.3 reduce-scatter.26
  344.3 32.9 reduce-scatter.28
  380.4 32.9 reduce-scatter.24
where the time goes:
time: 423 us; the launch traced here: 422 us
  waiting for transfers between devices  287 us (68%)
  starting transfers between devices  51.1 us (12%)
  matrix products  49.8 us (12%)
  between operations  14.5 us (3%)
  local copies, waits for them, and re-layouts  11.7 us (3%)
  other arithmetic  7.33 us (2%)
    unnamed x12, waiting for transfers between devices  124 us
    ppermute x8, waiting for transfers between devices, shifted(): return lax.ppermute(x, axis, pairs)  78.8 us
    reduce_scatter x2, waiting for transfers between devices, reduce_terms(): lax.psum_scatter(reordered[0].astype(jnp.bfloat16), 'seqlo', scatter_dime...  73.2 us
    ppermute x8, starting transfers between devices, shifted(): return lax.ppermute(x, axis, pairs)  50.4 us
    dot_general x6, matrix products, residual_block_backward(): lax.dot_general(moved[tap_index], conv_weight[tap_index * width:(tap_inde...  16.7 us
    dot_general x8, matrix products, contract_rows(): lax.dot_general(left, right, (((0,), (0,)), ((), ())), preferred_element_...  14.1 us
    reduce_scatter x2, waiting for transfers between devices, reduce_terms(): lax.psum_scatter(reordered[1].astype(jnp.bfloat16), 'seqlo', scatter_dime...  11.2 us
  transfers between devices with their start and end apart: 16, of which 11 were waited for; matrix products, arithmetic and copies ran while one was open for 14% of the time, Pallas kernels for 0%

commit v1 on v0

--- a/solution.py
+++ b/solution.py
@@ -93,7 +93,7 @@
     return (grad_in.astype(jnp.bfloat16), grad_conv, grad_proj)
 
 
-def per_device(
+def per_device_halo(
     tokens,
     cotangent,
     first_kernel_weight,
@@ -140,6 +140,60 @@
     )
 
 
+def local_shift(values, by):
+    padding = jnp.zeros((abs(by), values.shape[1]), values.dtype)
+    if by > 0:
+        return jnp.concatenate([padding, values[:-by]], 0)
+    return jnp.concatenate([values[-by:], padding], 0)
+
+
+def local_forward(x, conv, proj, step):
+    width = x.shape[1]
+    taps = (local_shift(x, step), x, local_shift(x, -step))
+    pre = sum(
+        jnp.dot(taps[k], conv[k * width : (k + 1) * width], preferred_element_type=jnp.float32)
+        for k in range(3)
+    )
+    inner = jax.nn.gelu(pre).astype(jnp.bfloat16)
+    mixed = lax.dot_general(inner, proj, (((1,), (1,)), ((), ())), preferred_element_type=jnp.float32)
+    return (x.astype(jnp.float32) + mixed).astype(jnp.bfloat16), pre, inner
+
+
+def local_backward(g, x, pre, inner, conv, proj, step):
+    width = g.shape[1]
+    grad_proj = contract_rows(g, inner)
+    _, pullback = jax.vjp(jax.nn.gelu, pre)
+    grad_pre = pullback(jnp.dot(g, proj, preferred_element_type=jnp.float32))[0].astype(jnp.bfloat16)
+    moved = (local_shift(grad_pre, -step), grad_pre, local_shift(grad_pre, step))
+    grad_conv = jnp.concatenate([contract_rows(x, m) for m in moved], 0)
+    gx = g.astype(jnp.float32)
+    for k in range(3):
+        gx = gx + lax.dot_general(
+            moved[k], conv[k * width : (k + 1) * width], (((1,), (1,)), ((), ())),
+            preferred_element_type=jnp.float32,
+        )
+    return gx.astype(jnp.bfloat16), grad_conv, grad_proj
+
+
+def per_device(tokens, cotangent, c1, p1, c2, p2):
+    outer = lax.axis_size("seqhi")
+    inner_count = lax.axis_size("seqlo")
+    rows = tokens.shape[0]
+    if rows * inner_count != FIRST_SPACING or rows % outer:
+        return per_device_halo(tokens, cotangent, c1, p1, c2, p2)
+    part = rows // outer
+    exchange = lambda a: lax.all_to_all(a, "seqhi", 0, 0, tiled=True)
+    x = exchange(tokens)
+    g = exchange(cotangent)
+    mid, pre1, inner1 = local_forward(x, c1, p1, part)
+    out, pre2, inner2 = local_forward(mid, c2, p2, part * (SECOND_SPACING // FIRST_SPACING))
+    gmid, gc2, gp2 = local_backward(g, mid, pre2, inner2, c2, p2, part * (SECOND_SPACING // FIRST_SPACING))
+    gx, gc1, gp1 = local_backward(gmid, x, pre1, inner1, c1, p1, part)
+    gc2, gp2 = reduce_terms((gc2, gp2))
+    gc1, gp1 = reduce_terms((gc1, gp1))
+    return exchange(out), exchange(gx), gc1, gp1, gc2, gp2
+
+
 def solution(mesh):
     placed = (P(("seqhi", "seqlo"), None), P(("seqhi", "seqlo"), None), P(), P(), P(), P())
     return jax.shard_map(

time: 423 us -> 352 us (0.83)
  waiting for transfers between devices: 287 us -> 212 us
  starting transfers between devices: 51.1 us -> 12.7 us
  blocking collectives: 0 us -> 26.3 us
  local copies, waits for them, and re-layouts: 11.7 us -> 24.1 us
    ppermute x8 -> x0, waiting for transfers between devices: 78.8 us -> none  [shifted(): return lax.ppermute(x, axis, pairs)]
    ppermute x8 -> x0, starting transfers between devices: 50.4 us -> none  [shifted(): return lax.ppermute(x, axis, pairs)]
    all_to_all x0 -> x1, blocking collectives: none -> 26.3 us  [per_device(): exchange = lambda a: lax.all_to_all(a, 'seqhi', 0, 0, tiled=True)]
    unnamed x12, waiting for transfers between devices: 124 us -> 138 us
    all_to_all x0 -> x3, waiting for transfers between devices: none -> 13.6 us  [per_device(): exchange = lambda a: lax.all_to_all(a, 'seqhi', 0, 0, tiled=True)]
    reduce_scatter x2, waiting for transfers between devices: 73.2 us -> 60.7 us  [reduce_terms(): lax.psum_scatter(reordered[0].astype(jnp.bfloat16), 'seqlo', scatter_dime...]
    all_to_all x0 -> x3, starting transfers between devices: none -> 12.2 us  [per_device(): exchange = lambda a: lax.all_to_all(a, 'seqhi', 0, 0, tiled=True)]
    reduce_scatter x2, waiting for transfers between devices: 11.2 us -> 0.01 us  [reduce_terms(): lax.psum_scatter(reordered[1].astype(jnp.bfloat16), 'seqlo', scatter_dime...]
  transfers between devices with their start and end apart: 16 -> 11, of which waited for: 11 -> 8; matrix products, arithmetic and copies ran while one was open for 14% -> 17% of each run, Pallas kernels for 0% -> 0%
where the time goes in v1:
time: 352 us; the launch traced here: 351 us
  waiting for transfers between devices  212 us (60%)
  matrix products  54 us (15%)
  blocking collectives  26.3 us (7%)
  local copies, waits for them, and re-layouts  24.1 us (7%)
  between operations  14.5 us (4%)
  starting transfers between devices  12.7 us (4%)
  other arithmetic  7.11 us (2%)
    unnamed x12, waiting for transfers between devices  138 us
    reduce_scatter x2, waiting for transfers between devices, reduce_terms(): lax.psum_scatter(reordered[0].astype(jnp.bfloat16), 'seqlo', scatter_dime...  60.7 us
    all_to_all x1, blocking collectives, per_device(): exchange = lambda a: lax.all_to_all(a, 'seqhi', 0, 0, tiled=True)  26.3 us
    dot_general x6, matrix products, local_backward(): lax.dot_general(moved[k], conv[k * width:(k + 1) * width], (((1,), (1,)),...  21.1 us
    all_to_all x3, waiting for transfers between devices, per_device(): exchange = lambda a: lax.all_to_all(a, 'seqhi', 0, 0, tiled=True)  13.6 us
    all_to_all x3, starting transfers between devices, per_device(): exchange = lambda a: lax.all_to_all(a, 'seqhi', 0, 0, tiled=True)  12.2 us
    dot_general x8, matrix products, contract_rows(): lax.dot_general(left, right, (((0,), (0,)), ((), ())), preferred_element_...  11.4 us
    dot_general x6, matrix products, local_forward(): jnp.dot(taps[k], conv[k * width:(k + 1) * width], preferred_element_type=...  10.2 us
  transfers between devices with their start and end apart: 11, of which 8 were waited for; matrix products, arithmetic and copies ran while one was open for 17% of the time, Pallas kernels for 0%

profile of v1, /device:TPU:0, one launch (start us, length us, event | category | flops | bytes accessed | tf_op | source)
XLA Modules:
  0.0 350.7 jit_solution(1886136509112466428)
XLA Ops:
  7.2 26.3 %all_to_all.48 = bf16[8,128,768]{2,1,0:T(8,128)(2,1)S(1)} all-to-all(bf16[8,128,768]{2,1,0:T(8,128)(2,1)} %bitcast.70), channel_id=1, replica_groups=mesh['seqhi'=8,'seqlo'=4] {'seqhi'}, dimensions={0} | all-to-all | bytes 3145728 | tf_op jit(solution)/shard_map/all_to_all | solution.py:185
  33.5 4.3 %all-to-all-start.2 = ((bf16[8,128,768]{2,1,0:T(8,128)(2,1)}), bf16[8,128,768]{2,1,0:T(8,128)(2,1)}, u32[]{:S(2)}, u32[]{:S(2)}) async-start(bf16[8,128,768]{2,1,0:T(8,128)(2,1)} %bitcast.71), calls=%async_computation.2 | async-start | bytes 3145728 | tf_op jit(solution)/shard_map/all_to_all | solution.py:185
  37.8 0.0 reduce-scatter.23.cloned.1.call-start
  37.8 2.0 fusion.52
  39.9 0.3 fusion.69
  40.2 1.2 copy-done.6
  41.3 1.0 fusion.18
  42.3 1.0 add_add_fusion.1
  43.4 1.2 copy-done.14
  44.5 1.3 add_convert_fusion.3
  45.8 1.2 fusion.68
  47.0 1.3 copy-done.12
  48.3 2.1 fusion.14
  50.4 2.2 fusion.44
  52.6 6.2 %all-to-all-done.2 = bf16[8,128,768]{2,1,0:T(8,128)(2,1)} async-done(((bf16[8,128,768]{2,1,0:T(8,128)(2,1)}), bf16[8,128,768]{2,1,0:T(8,128)(2,1)}, u32[]{:S(2)}, u32[]{:S(2)}) %all-to-all-start.2) | async-done | bytes 1572896 | tf_op jit(solution)/shard_map/all_to_all | solution.py:185
  58.8 2.5 fusion.72
  61.4 0.2 copy-done.19
  61.5 0.5 copy-done.20
  62.0 1.9 fusion.13
  63.9 1.2 fusion.71
  65.2 2.6 fusion.42
  67.8 3.2 fusion.29
  71.0 1.4 copy.30
  72.4 0.9 copy.31
  73.3 0.2 reduce-scatter.19.cloned.1.call-start
  73.6 2.4 fusion.33
  76.0 2.7 add_convert_fusion.1
  78.7 1.1 convolution_convert_fusion.4
  79.8 0.1 copy-done.2
  79.9 0.9 copy.28
  80.9 2.7 convolution_convert_fusion.1
  83.6 1.0 convolution_convert_fusion.3
  84.6 1.0 convolution_convert_fusion.2
  85.6 0.2 pad_maximum_fusion.1
  85.8 1.4 copy.29
  87.3 3.6 %fusion.6 = bf16[1024,384]{1,0:T(8,128)(2,1)S(1)} fusion(f32[1024,384]{1,0:T(8,128)} %copy-done.14, bf16[1024,768]{1,0:T(8,128)(2,1)} %copy-done.2, bf16[768,384]{1,0:T(8,128)(2,1)S(1)} %copy-done), kind=kOutput, calls=%fused_computation.16 | convolution fusion | flops 611844096 | bytes 4521984 | tf_op jit(solution)/shard_map/dot_general | solution.py:166
  90.9 0.1 fusion.70
  91.1 0.8 fusion.28
  91.9 0.3 copy-done.7
  92.2 0.8 fusion.26
  93.0 0.8 fusion.27
  93.8 1.3 pad_maximum_fusion
  95.2 3.9 %copy.26 = bf16[2304,384]{1,0:T(8,128)(2,1)} copy(bf16[2304,384]{0,1:T(8,128)(2,1)} %pad_maximum_fusion) | data formatting | bytes 3538944 | tf_op jit(solution)/shard_map/concatenate | solution.py:168
  99.0 3.0 copy.27
  102.0 1.4 copy-done.5
  103.4 3.8 %add_convert_fusion.2 = bf16[1024,768]{1,0:T(8,128)(2,1)} fusion(bf16[1024,768]{1,0:T(8,128)(2,1)S(1)} %copy-done.5, bf16[768,384]{1,0:T(8,128)(2,1)S(1)} %copy-done.18, f32[1024,384]{1,0:T(8,128)} %copy-done.21), kind=kOutput, calls=%fused_computation.2 | convolution fusion | flops 609878016 | bytes 5308416 | tf_op jit(solution)/shard_map/dot_general | solution.py:158
  107.2 3.6 %all-to-all-start.1 = ((bf16[8,128,768]{2,1,0:T(8,128)(2,1)}), bf16[8,128,768]{2,1,0:T(8,128)(2,1)S(1)}, u32[]{:S(2)}, u32[]{:S(2)}) async-start(bf16[8,128,768]{2,1,0:T(8,128)(2,1)} %bitcast.72), calls=%async_computation.1 | async-start | bytes 3145728 | tf_op jit(solution)/shard_map/all_to_all | solution.py:185
  110.8 3.7 %fusion.50 = f32[1024,768]{1,0:T(8,128)} fusion(bf16[1024,384]{1,0:T(8,128)(2,1)S(1)} %fusion.6, bf16[2304,384]{1,0:T(8,128)(2,1)} %param.8), kind=kOutput, calls=%fused_computation.68 | convolution fusion | flops 603979776 | bytes 4521984 | tf_op jit(solution)/shard_map/dot_general | solution.py:171
  114.6 4.0 %fusion.38 = f32[1024,768]{1,0:T(8,128)} fusion(bf16[896,384]{1,0:T(8,128)(2,1)} %copy-done.7, bf16[2304,384]{1,0:T(8,128)(2,1)} %param.8), kind=kOutput, calls=%fused_computation.56 | convolution fusion | flops 603979776 | bytes 4423680 | tf_op jit(solution)/shard_map/dot_general | solution.py:171
  118.7 5.6 %add_convert_fusion = bf16[1024,768]{1,0:T(8,128)(2,1)} fusion(f32[1024,768]{1,0:T(8,128)} %fusion.50, f32[1024,768]{1,0:T(8,128)} %fusion.38, bf16[1024,768]{1,0:T(8,128)(2,1)} %copy-done.2, bf16[896,384]{1,0:T(8,128)(2,1)S(1)} %copy-done.9, bf16[2304,384]{1,0:T(8,128)(2,1)} %param.8), kind=kOutput, calls=%fused_computation | convolution fusion | flops 607911936 | bytes 10715136 | tf_op jit(solution)/shard_map/dot_general | solution.py:171
  124.3 7.4 %all-to-all-done.1 = bf16[8,128,768]{2,1,0:T(8,128)(2,1)S(1)} async-done(((bf16[8,128,768]{2,1,0:T(8,128)(2,1)}), bf16[8,128,768]{2,1,0:T(8,128)(2,1)S(1)}, u32[]{:S(2)}, u32[]{:S(2)}) %all-to-all-start.1) | async-done | bytes 1572896 | tf_op jit(solution)/shard_map/all_to_all | solution.py:185
  131.7 4.3 %all-to-all-start.3 = ((bf16[8,128,768]{2,1,0:T(8,128)(2,1)}), bf16[8,128,768]{2,1,0:T(8,128)(2,1)}, u32[]{:S(2)}, u32[]{:S(2)}) async-start(bf16[8,128,768]{2,1,0:T(8,128)(2,1)} %bitcast.65), calls=%async_computation.3 | async-start | bytes 3145728 | tf_op jit(solution)/shard_map/all_to_all | solution.py:185
  136.1 21.1 %reduce-scatter.21.cloned.1.call-done = bf16[576,384]{1,0:T(8,128)(2,1)} async-done(((bf16[2304,384]{1,0:T(8,128)(2,1)}), bf16[576,384]{1,0:T(8,128)(2,1)}) %reduce-scatter.21.cloned.1.call-update) | async-done | bytes 442384 | tf_op jit(solution)/shard_map/reduce_scatter | solution.py:55
  157.2 39.6 %reduce-scatter.17.cloned.1.call-done = bf16[576,384]{1,0:T(8,128)(2,1)} async-done(((bf16[2304,384]{1,0:T(8,128)(2,1)}), bf16[576,384]{1,0:T(8,128)(2,1)}) %reduce-scatter.17.cloned.1.call-update) | async-done | bytes 442384 | tf_op jit(solution)/shard_map/reduce_scatter | solution.py:55
  196.9 34.3 %reduce-scatter.31.cloned.1.call-done = bf16[24,384]{1,0:T(8,128)(2,1)} async-done(((bf16[192,384]{1,0:T(8,128)(2,1)}), bf16[24,384]{1,0:T(8,128)(2,1)}) %reduce-scatter.31.cloned.1.call-update) | async-done | bytes 18448
  231.2 1.3 convert_element_type.133
  232.5 34.0 %reduce-scatter.27.cloned.1.call-done = bf16[24,384]{1,0:T(8,128)(2,1)} async-done(((bf16[192,384]{1,0:T(8,128)(2,1)}), bf16[24,384]{1,0:T(8,128)(2,1)}) %reduce-scatter.27.cloned.1.call-update) | async-done | bytes 18448
  266.6 1.3 convert_element_type.123
  267.9 34.7 %reduce-scatter.29.cloned.1.call-done = bf16[72,384]{1,0:T(8,128)(2,1)} async-done(((bf16[576,384]{1,0:T(8,128)(2,1)}), bf16[72,384]{1,0:T(8,128)(2,1)}) %reduce-scatter.29.cloned.1.call-update) | async-done | bytes 55312
  302.6 1.5 convert_element_type.127
  304.1 34.6 %reduce-scatter.25.cloned.1.call-done = bf16[72,384]{1,0:T(8,128)(2,1)} async-done(((bf16[576,384]{1,0:T(8,128)(2,1)}), bf16[72,384]{1,0:T(8,128)(2,1)}) %reduce-scatter.25.cloned.1.call-update) | async-done | bytes 55312
  338.6 1.5 convert_element_type.118
  340.1 1.1 copy.34
  341.3 2.7 copy.35
  (53 shorter events, 0.5 us)
Async XLA Ops:
  7.2 37.4 %copy-start = (bf16[768,384]{1,0:T(8,128)(2,1)S(1)}, bf16[768,384]{1,0:T(8,128)(2,1)}, u32[]{:S(2)}) copy-start(bf16[768,384]{1,0:T(8,128)(2,1)} %param.9) | copy-start | bytes 1769476
  33.5 25.3 %all-to-all-start.2 = ((bf16[8,128,768]{2,1,0:T(8,128)(2,1)}), bf16[8,128,768]{2,1,0:T(8,128)(2,1)}, u32[]{:S(2)}, u32[]{:S(2)}) async-start(bf16[8,128,768]{2,1,0:T(8,128)(2,1)} %bitcast.71), calls=%async_computation.2 | async-start | bytes 3145728 | tf_op jit(solution)/shard_map/all_to_all | solution.py:185
  37.8 76.8 %reduce-scatter.23.cloned.1.call-start = ((), (), s32[]{:S(2)}) async-start(), calls=%async_computation.15 | async-start | bytes 737280 | tf_op jit(solution)/shard_map/reduce_scatter | solution.py:58
  39.9 1.5 copy-start.6
  43.3 1.2 copy-start.14
  45.8 4.6 %copy-start.3 = (bf16[1024,768]{1,0:T(8,128)(2,1)}, bf16[1024,768]{1,0:T(8,128)(2,1)S(1)}, u32[]{:S(2)}) copy-start(bf16[1024,768]{1,0:T(8,128)(2,1)S(1)} %add_convert_fusion.3) | copy-start | bytes 4718596
  45.8 2.5 copy-start.12
  50.4 8.4 %copy-start.17 = (bf16[768,384]{1,0:T(8,128)(2,1)S(1)}, bf16[768,384]{1,0:T(8,128)(2,1)}, u32[]{:S(2)}) copy-start(bf16[768,384]{1,0:T(8,128)(2,1)} %param.11) | copy-start | bytes 1769476
  58.8 2.6 copy-start.13
  58.8 2.6 copy-start.16
  58.8 2.8 copy-start.19
  58.8 3.2 copy-start.20
  63.9 3.9 %copy-start.21 = (f32[1024,384]{1,0:T(8,128)}, f32[1024,384]{1,0:T(8,128)S(1)}, u32[]{:S(2)}) copy-start(f32[1024,384]{1,0:T(8,128)S(1)} %get-tuple-element.15) | copy-start | bytes 4718596
  73.3 45.3 %reduce-scatter.19.cloned.1.call-start = ((), (), s32[]{:S(2)}) async-start(), calls=%async_computation.13 | async-start | bytes 737280 | tf_op jit(solution)/shard_map/reduce_scatter | solution.py:58
  73.6 2.4 copy-start.1
  73.6 2.4 copy-start.11
  76.0 2.7 copy-start.15
  78.7 1.2 copy-start.2
  80.8 2.8 copy-start.10
  80.8 76.3 %reduce-scatter.21.cloned.1.call-start = ((), (), s32[]{:S(2)}) async-start(), calls=%async_computation.14 | async-start | bytes 2211840 | tf_op jit(solution)/shard_map/reduce_scatter | solution.py:55
  80.9 2.7 copy-start.4
  87.2 109.6 %reduce-scatter.17.cloned.1.call-start = ((), (), s32[]{:S(2)}) async-start(), calls=%async_computation.12 | async-start | bytes 2211840 | tf_op jit(solution)/shard_map/reduce_scatter | solution.py:55
  91.0 0.9 copy-start.8
  91.1 1.1 copy-start.7
  99.0 3.0 copy-start.18
  102.0 1.4 copy-start.5
  107.2 24.5 %all-to-all-start.1 = ((bf16[8,128,768]{2,1,0:T(8,128)(2,1)}), bf16[8,128,768]{2,1,0:T(8,128)(2,1)S(1)}, u32[]{:S(2)}, u32[]{:S(2)}) async-start(bf16[8,128,768]{2,1,0:T(8,128)(2,1)} %bitcast.72), calls=%async_computation.1 | async-start | bytes 3145728 | tf_op jit(solution)/shard_map/all_to_all | solution.py:185
  110.8 120.4 %reduce-scatter.31.cloned.1.call-start = ((), (), s32[]{:S(2)}) async-start(), calls=%async_computation.19 | async-start | bytes 165888
  114.6 4.1 %copy-start.9 = (bf16[896,384]{1,0:T(8,128)(2,1)S(1)}, bf16[896,384]{1,0:T(8,128)(2,1)}, u32[]{:S(2)}) copy-start(bf16[896,384]{1,0:T(8,128)(2,1)} %copy-done.8) | copy-start | bytes 2064388
  114.6 152.0 %reduce-scatter.27.cloned.1.call-start = ((), (), s32[]{:S(2)}) async-start(), calls=%async_computation.17 | async-start | bytes 165888
  131.7 65.1 %all-to-all-start.3 = ((bf16[8,128,768]{2,1,0:T(8,128)(2,1)}), bf16[8,128,768]{2,1,0:T(8,128)(2,1)}, u32[]{:S(2)}, u32[]{:S(2)}) async-start(bf16[8,128,768]{2,1,0:T(8,128)(2,1)} %bitcast.65), calls=%async_computation.3 | async-start | bytes 3145728 | tf_op jit(solution)/shard_map/all_to_all | solution.py:185
  136.0 166.6 %reduce-scatter.29.cloned.1.call-start = ((), (), s32[]{:S(2)}) async-start(), calls=%async_computation.18 | async-start | bytes 497664
  157.2 181.5 %reduce-scatter.25.cloned.1.call-start = ((), (), s32[]{:S(2)}) async-start(), calls=%async_computation.16 | async-start | bytes 497664
Sparse Core Ops, SparseCore 0:
  73.4 21.5 reduce-scatter.22
  97.3 20.5 reduce-scatter.18
  120.2 36.8 reduce-scatter.20
  159.3 37.4 reduce-scatter.16
  199.7 31.4 reduce-scatter.30
  234.1 32.4 reduce-scatter.26
  269.7 32.8 reduce-scatter.28
  305.7 32.8 reduce-scatter.24

commit v2 on v0

--- a/solution.py
+++ b/solution.py
@@ -1,6 +1,11 @@
+import functools
+import math
+
 import jax
 import jax.numpy as jnp
 from jax import lax
+from jax.experimental import pallas as pl
+from jax.experimental.pallas import tpu as pltpu
 from jax.sharding import PartitionSpec as P
 
 FIRST_SPACING = 4096
@@ -93,7 +98,7 @@
     return (grad_in.astype(jnp.bfloat16), grad_conv, grad_proj)
 
 
-def per_device(
+def per_device_halo(
     tokens,
     cotangent,
     first_kernel_weight,
@@ -140,6 +145,269 @@
     )
 
 
+CHUNKS = 4
+MESH = pl.DeviceIdType.MESH
+F32 = jnp.float32
+BF16 = jnp.bfloat16
+WEIGHT = {"y": 16, "x": 8, "c": 4, "z1": 2, "z0": 1}
+ORDERS = (("c", "z0", "z1", "x", "y"), ("c", "x", "y", "z0", "z1"))
+
+
+def gelu_pair(v):
+    scale = math.sqrt(2.0 / math.pi)
+    square = v * v
+    t = jnp.tanh(scale * v * (1.0 + 0.044715 * square))
+    half = 0.5 * (1.0 + t)
+    slope = half + 0.5 * v * (1.0 - t * t) * (scale * (1.0 + 3 * 0.044715 * square))
+    return v * half, slope
+
+
+def moved_down(a, by):
+    return jnp.concatenate([jnp.zeros((by, a.shape[1]), a.dtype), a[: a.shape[0] - by]], 0)
+
+
+def moved_up(a, by):
+    return jnp.concatenate([a[by:], jnp.zeros((by, a.shape[1]), a.dtype)], 0)
+
+
+def nt(a, b):
+    return lax.dot_general(a, b, (((1,), (1,)), ((), ())), preferred_element_type=F32)
+
+
+def tn(a, b):
+    return lax.dot_general(a, b, (((0,), (0,)), ((), ())), preferred_element_type=F32)
+
+
+def mega(
+    n, part, steps,
+    tok, cot, c1, p1, c2, p2,
+    out, gx, gc1, gp1, gc2, gp2,
+    xs, gs, os, gxs, w1, q1, w2, q2, mid_s, in1, in2, d1, d2, ac1, ap1, ac2, ap2,
+    b0s, b0r, b1s, b1r, b2s, b2r, b3s, b3r, b4s, b4r,
+    ssem, rsem, lsem, wsem, zs, zr,
+):
+    me = lax.axis_index("seqhi")
+    lo = lax.axis_index("seqlo")
+    q = part // CHUNKS
+    width = tok.shape[1]
+    inner = w1.shape[1] // 3
+    rows = n * q
+
+    loads = []
+    for k in range(3):
+        for b, (src, dst) in enumerate(((c1, w1), (c2, w2))):
+            loads.append(pltpu.make_async_copy(
+                src.at[pl.ds(k * width, width), :],
+                dst.at[:, pl.ds(k * inner, inner)], wsem.at[2 * k + b]))
+    loads.append(pltpu.make_async_copy(p1, q1, wsem.at[6]))
+    loads.append(pltpu.make_async_copy(p2, q2, wsem.at[7]))
+    for load in loads:
+        load.start()
+
+    barrier = pltpu.get_barrier_semaphore()
+
+    def greet(d, carry):
+        pl.semaphore_signal(barrier, inc=1, device_id=(lax.rem(me + d, n), lo), device_id_type=MESH)
+        return carry
+
+    lax.fori_loop(1, n, greet, 0)
+    z0, z1 = lax.rem(lo, 2), lo // 2
+    near, far = lo + 1 - 2 * z0, lo + 2 - 4 * z1
+    pl.semaphore_signal(barrier, inc=1, device_id=(me, near), device_id_type=MESH)
+    pl.semaphore_signal(barrier, inc=1, device_id=(me, far), device_id_type=MESH)
+    pl.semaphore_wait(barrier, n + 1)
+
+    def span(owner, c):
+        return pl.ds(pl.multiple_of(owner * part + c * q, 16), q)
+
+    def inbound(a, c, peer, slot):
+        src, dst = ((tok, xs), (cot, gs))[a]
+        return pltpu.make_async_remote_copy(
+            src_ref=src.at[span(peer, c), :], dst_ref=dst.at[c, slot],
+            send_sem=ssem.at[a, c, peer], recv_sem=rsem.at[a, c, slot],
+            device_id=(peer, lo), device_id_type=MESH)
+
+    def outbound(a, c, peer, owner):
+        src, dst = ((os, out), (gxs, gx))[a]
+        return pltpu.make_async_remote_copy(
+            src_ref=src.at[c, peer], dst_ref=dst.at[span(owner, c), :],
+            send_sem=ssem.at[2 + a, c, peer], recv_sem=rsem.at[2 + a, c, owner],
+            device_id=(peer, lo), device_id_type=MESH)
+
+    def own_in(a, c):
+        src, dst = ((tok, xs), (cot, gs))[a]
+        return pltpu.make_async_copy(src.at[span(me, c), :], dst.at[c, me], lsem.at[a, c])
+
+    def own_out(a, c):
+        src, dst = ((os, out), (gxs, gx))[a]
+        return pltpu.make_async_copy(src.at[c, me], dst.at[span(me, c), :], lsem.at[2 + a, c])
+
+    def peers(body):
+        def step(d, carry):
+            body(lax.rem(me + d, n))
+            return carry
+        lax.fori_loop(1, n, step, 0)
+
+    def send_chunk(c, carry):
+        for a in range(2):
+            own_in(a, c).start()
+            peers(lambda peer: inbound(a, c, peer, me).start())
+        return carry
+
+    lax.fori_loop(0, CHUNKS, send_chunk, 0)
+    for ref in (ac1, ap1, ac2, ap2):
+        ref[...] = jnp.zeros(ref.shape, F32)
+    for load in loads:
+        load.wait()
+
+    def forward(x, w, p, hid, slope, by):
+        a = jnp.dot(x, w[...], preferred_element_type=F32)
+        pre = a[:, inner : 2 * inner] + moved_down(a[:, :inner], by) + moved_up(a[:, 2 * inner :], by)
+        value, slope[...] = gelu_pair(pre)
+        hid[...] = value.astype(BF16)
+        return (x.astype(F32) + nt(hid[...], p[...])).astype(BF16)
+
+    def backward(g, x, w, p, hid, slope, by, ac, ap):
+        ap[...] += tn(g, hid[...])
+        grad = (jnp.dot(g, p[...], preferred_element_type=F32) * slope[...]).astype(BF16)
+        moved = jnp.concatenate([moved_up(grad, by), grad, moved_down(grad, by)], 1)
+        gc = tn(x, moved)
+        for k in range(3):
+            ac[pl.ds(k * width, width), :] += gc[:, k * inner : (k + 1) * inner]
+        return (g.astype(F32) + nt(moved, w[...])).astype(BF16)
+
+    def chunk(c, carry):
+        own_in(0, c).wait()
+        peers(lambda peer: inbound(0, c, peer, peer).wait_recv())
+        mid_s[...] = forward(xs[c].reshape(rows, width), w1, q1, in1, d1, q)
+        os[c] = forward(mid_s[...], w2, q2, in2, d2, steps * q).reshape(n, q, width)
+        own_out(0, c).start()
+        peers(lambda peer: outbound(0, c, peer, me).start())
+        own_in(1, c).wait()
+        peers(lambda peer: inbound(1, c, peer, peer).wait_recv())
+        gmid = backward(gs[c].reshape(rows, width), mid_s[...], w2, q2, in2, d2, steps * q, ac2, ap2)
+        gxs[c] = backward(gmid, xs[c].reshape(rows, width), w1, q1, in1, d1, q, ac1, ap1).reshape(n, q, width)
+        own_out(1, c).start()
+        peers(lambda peer: outbound(1, c, peer, me).start())
+        return carry
+
+    lax.fori_loop(0, CHUNKS, chunk, 0)
+
+    bit = {"c": lax.rem(me, 2), "x": lax.rem(me // 2, 2), "y": me // 4, "z0": z0, "z1": z1}
+    hop = {"c": 1, "x": 2, "y": 4}
+    partner = {name: (me + hop[name] - 2 * hop[name] * bit[name], lo) for name in hop}
+    partner["z0"], partner["z1"] = (me, near), (me, far)
+    sums = ((ac2, ap2), (ac1, ap1))
+    sends, recvs = (b0s, b1s, b2s, b3s, b4s), (b0r, b1r, b2r, b3r, b4r)
+    cr, pr = ac1.shape[0] // 32, ap1.shape[0] // 32
+
+    def piece(b, p):
+        conv, proj = sums[b]
+        return conv.at[pl.ds(pl.multiple_of(p * cr, 8), cr), :], proj.at[pl.ds(pl.multiple_of(p * pr, 8), pr), :]
+
+    def address(b, s, m, flip):
+        order = ORDERS[b]
+        p = 0
+        for t, name in enumerate(order):
+            w = WEIGHT[name]
+            if t < s:
+                p = p + bit[name] * w
+            elif t == s:
+                p = p + ((1 - bit[name]) if flip else bit[name]) * w
+            else:
+                p = p + lax.rem(m // (1 << (4 - t)), 2) * w
+        return p
+
+    def exchange(b, s):
+        return pltpu.make_async_remote_copy(
+            src_ref=sends[s].at[b], dst_ref=recvs[s].at[b], send_sem=zs.at[b, s], recv_sem=zr.at[b, s],
+            device_id=partner[ORDERS[b][s]], device_id_type=MESH)
+
+    def arrived(b, s, m, flip):
+        got = recvs[s - 1][b, ((1 - bit[ORDERS[b][s]]) if flip else bit[ORDERS[b][s]]) * (1 << (4 - s)) + m]
+        return got.astype(F32)
+
+    for s in range(5):
+        count = 1 << (4 - s)
+        for b in range(2):
+            if s:
+                exchange(b, s - 1).wait_recv()
+
+            def give(m, carry):
+                conv, proj = piece(b, address(b, s, m, True))
+                value = jnp.concatenate([conv[...], proj[...]], 0)
+                if s:
+                    value = value + arrived(b, s, m, True)
+                sends[s][b, m] = value.astype(BF16)
+                return carry
+
+            lax.fori_loop(0, count, give, 0)
+            exchange(b, s).start()
+        if s:
+            for b in range(2):
+                def keep(m, carry):
+                    conv, proj = piece(b, address(b, s, m, False))
+                    got = arrived(b, s, m, False)
+                    conv[...] += got[:cr]
+                    proj[...] += got[cr:]
+                    return carry
+
+                lax.fori_loop(0, count, keep, 0)
+    for b, (conv_out, proj_out) in enumerate(((gc2, gp2), (gc1, gp1))):
+        exchange(b, 4).wait_recv()
+        conv, proj = piece(b, address(b, 5, 0, False))
+        got = recvs[4][b, 0].astype(F32)
+        conv_out[...] = conv[...] + got[:cr]
+        proj_out[...] = proj[...] + got[cr:]
+        for s in range(5):
+            exchange(b, s).wait_send()
+
+    def drain(c, carry):
+        for a in range(2):
+            own_out(a, c).wait()
+            peers(lambda peer: inbound(a, c, peer, me).wait_send())
+            peers(lambda peer: outbound(a, c, peer, me).wait_send())
+            peers(lambda peer: outbound(a, c, peer, peer).wait_recv())
+        return carry
+
+    lax.fori_loop(0, CHUNKS, drain, 0)
+
+
+def per_device(tokens, cotangent, c1, p1, c2, p2):
+    n = lax.axis_size("seqhi")
+    inner_count = lax.axis_size("seqlo")
+    rows, width = tokens.shape
+    inner = p1.shape[1]
+    pieces = n * inner_count
+    if rows * inner_count != FIRST_SPACING or (n, inner_count) != (8, 4) or rows % (n * CHUNKS * 16):
+        return per_device_halo(tokens, cotangent, c1, p1, c2, p2)
+    part = rows // n
+    q = part // CHUNKS
+    slots = pltpu.VMEM((CHUNKS, n, q, width), BF16)
+    tile = (c1.shape[0] + p1.shape[0]) // pieces
+    scratch = [slots] * 4
+    scratch += [pltpu.VMEM((width, 3 * inner), BF16), pltpu.VMEM((width, inner), BF16)] * 2
+    scratch += [pltpu.VMEM((n * q, width), BF16)]
+    scratch += [pltpu.VMEM((n * q, inner), BF16)] * 2 + [pltpu.VMEM((n * q, inner), F32)] * 2
+    scratch += [pltpu.VMEM(c1.shape, F32), pltpu.VMEM(p1.shape, F32)] * 2
+    for s in range(5):
+        scratch += [pltpu.VMEM((2, 1 << (4 - s), tile, inner), BF16)] * 2
+    scratch += [pltpu.SemaphoreType.DMA((4, CHUNKS, n))] * 2
+    scratch += [pltpu.SemaphoreType.DMA((4, CHUNKS)), pltpu.SemaphoreType.DMA((8,))]
+    scratch += [pltpu.SemaphoreType.DMA((2, 5))] * 2
+    grads = [(a.shape[0] // pieces, inner) for a in (c1, p1, c2, p2)]
+    return pl.pallas_call(
+        functools.partial(mega, n, part, SECOND_SPACING // FIRST_SPACING),
+        out_shape=[jax.ShapeDtypeStruct(tokens.shape, BF16)] * 2
+        + [jax.ShapeDtypeStruct(g, F32) for g in grads],
+        in_specs=[pl.BlockSpec(memory_space=pl.ANY)] * 6,
+        out_specs=[pl.BlockSpec(memory_space=pl.ANY)] * 2 + [pl.BlockSpec(memory_space=pltpu.VMEM)] * 4,
+        scratch_shapes=scratch,
+        compiler_params=pltpu.CompilerParams(
+            collective_id=0, has_side_effects=True, vmem_limit_bytes=60 * 1024 * 1024),
+    )(tokens, cotangent, c1, p1, c2, p2)
+
+
 def solution(mesh):
     placed = (P(("seqhi", "seqlo"), None), P(("seqhi", "seqlo"), None), P(), P(), P(), P())
     return jax.shard_map(

time: 423 us -> 117 us (0.28)
  waiting for transfers between devices: 287 us -> 0 us
  Pallas kernels: 0 us -> 110 us
  starting transfers between devices: 51.1 us -> 0 us
  matrix products: 49.8 us -> 0 us
  between operations: 14.5 us -> 0.67 us
  other arithmetic: 7.33 us -> 0 us
  local copies, waits for them, and re-layouts: 11.7 us -> 6.46 us
    unnamed x12 -> x0, waiting for transfers between devices: 124 us -> none
    pallas_call x0 -> x1, Pallas kernels: none -> 110 us  [per_device(): pl.pallas_call(functools.partial(mega, n, part, SECOND_SPACING // FIRST_S...]
    reduce_scatter x4 -> x0, waiting for transfers between devices: 84.4 us -> none  [the longest x2 73.2 us: reduce_terms(): lax.psum_scatter(reordered[0].astype(jnp.bfloat16), 'seqlo', scatter_dime...]
    ppermute x8 -> x0, waiting for transfers between devices: 78.8 us -> none  [shifted(): return lax.ppermute(x, axis, pairs)]
    ppermute x8 -> x0, starting transfers between devices: 50.4 us -> none  [shifted(): return lax.ppermute(x, axis, pairs)]
    dot_general x24 -> x0, matrix products: 49.8 us -> none  [the longest x6 16.7 us: residual_block_backward(): lax.dot_general(moved[tap_index], conv_weight[tap_index * width:(tap_inde...]
    convert_element_type x5 -> x0, local copies, waits for them, and re-layouts: 6.39 us -> none  [the longest x2 4.28 us: reduce_terms(): reordered[0].astype(jnp.bfloat16)]
    convert_element_type x4 -> x0, other arithmetic: 5.61 us -> none  [reduce_terms(): return (lax.psum_scatter(partial_sums[0].astype(jnp.bfloat16), 'seqhi', s...]
  transfers between devices with their start and end apart: 16 -> 0, of which waited for: 11 -> 0; matrix products, arithmetic and copies ran while one was open for 14% -> 0% of each run, Pallas kernels for 0% -> 0%
where the time goes in v2:
time: 117 us
  Pallas kernels  110 us (94%)
  local copies, waits for them, and re-layouts  6.46 us (6%)
    pallas_call x1, Pallas kernels, per_device(): pl.pallas_call(functools.partial(mega, n, part, SECOND_SPACING // FIRST_S...  110 us
    unnamed x16, local copies, waits for them, and re-layouts  6.46 us

profile of v2, /device:TPU:0, one launch (start us, length us, event | category | flops | bytes accessed | tf_op | source)
XLA Modules:
  0.0 116.7 jit_solution(7051942335317234034)
XLA Ops:
  0.6 109.6 %shard_map.109 = (bf16[1024,768]{1,0:T(8,128)(2,1)}, bf16[1024,768]{1,0:T(8,128)(2,1)}, f32[72,384]{1,0:T(8,128)}, f32[24,384]{1,0:T(8,128)}, f32[72,384]{1,0:T(8,128)}, /*index=5*/f32[24,384]{1,0:T(8,128)}) custom-call(bf16[1024,768]{1,0:T(8,128)(2,1)} %tok.1, bf16[1024,768]{1,0:T(8,128)(2,1)} %cot.1, bf16[2304,384]{1,0:T(8,128)(2,1)} %c1.1, ...), custom_call_target="tpu_custom_call" | custom-call | tf_op jit(solution)/shard_map/pallas_call | solution.py:399
  110.2 0.0 copy-start
  110.2 2.8 %copy.18 = bf16[1024,768]{1,0:T(8,128)(2,1)} copy(bf16[1024,768]{1,0:T(8,128)(2,1)} %get-tuple-element.12) | data formatting | bytes 3145728
  113.0 0.0 copy-done
  113.0 0.0 copy-start.2
  113.0 0.0 copy-start.4
  113.0 0.0 copy-start.1
  113.0 0.0 copy-start.3
  113.0 1.1 copy.19
  114.1 0.0 copy-done.2
  114.1 0.6 copy.20
  114.8 0.0 copy-done.4
  114.8 0.6 copy.21
  115.4 0.0 copy-done.1
  115.4 0.6 copy.22
  116.1 0.0 copy-done.3
  116.1 0.6 copy.23
Async XLA Ops:
  110.2 2.8 %copy-start = (bf16[1024,768]{1,0:T(8,128)(2,1)S(1)}, bf16[1024,768]{1,0:T(8,128)(2,1)}, u32[]{:S(2)}) copy-start(bf16[1024,768]{1,0:T(8,128)(2,1)} %get-tuple-element.13) | copy-start | bytes 4718596
  113.0 1.2 %copy-start.2 = (f32[72,384]{1,0:T(8,128)S(1)}, f32[72,384]{1,0:T(8,128)}, u32[]{:S(2)}) copy-start(f32[72,384]{1,0:T(8,128)} %get-tuple-element.14) | copy-start | bytes 331780
  113.0 1.8 %copy-start.4 = (f32[24,384]{1,0:T(8,128)S(1)}, f32[24,384]{1,0:T(8,128)}, u32[]{:S(2)}) copy-start(f32[24,384]{1,0:T(8,128)} %get-tuple-element.15) | copy-start | bytes 110596
  113.0 2.4 %copy-start.1 = (f32[72,384]{1,0:T(8,128)S(1)}, f32[72,384]{1,0:T(8,128)}, u32[]{:S(2)}) copy-start(f32[72,384]{1,0:T(8,128)} %get-tuple-element.16) | copy-start | bytes 331780
  113.0 3.1 %copy-start.3 = (f32[24,384]{1,0:T(8,128)S(1)}, f32[24,384]{1,0:T(8,128)}, u32[]{:S(2)}) copy-start(f32[24,384]{1,0:T(8,128)} %get-tuple-element.17) | copy-start | bytes 110596

commit v3 on v2

--- a/solution.py
+++ b/solution.py
@@ -146,6 +146,8 @@
 
 
 CHUNKS = 4
+AT_ONCE = 2
+LATE = {1: (2,), 2: (3,)}
 MESH = pl.DeviceIdType.MESH
 F32 = jnp.float32
 BF16 = jnp.bfloat16
@@ -243,8 +245,8 @@
         return pltpu.make_async_copy(src.at[c, me], dst.at[span(me, c), :], lsem.at[2 + a, c])
 
     def peers(body):
-        def step(d, carry):
-            body(lax.rem(me + d, n))
+        def step(i, carry):
+            body(lax.rem(me + i, n))
             return carry
         lax.fori_loop(1, n, step, 0)
 
@@ -276,19 +278,21 @@
             ac[pl.ds(k * width, width), :] += gc[:, k * inner : (k + 1) * inner]
         return (g.astype(F32) + nt(moved, w[...])).astype(BF16)
 
+    def ship(a, c):
+        own_out(a, c).start()
+        peers(lambda peer: outbound(a, c, peer, me).start())
+
     def chunk(c, carry):
         own_in(0, c).wait()
         peers(lambda peer: inbound(0, c, peer, peer).wait_recv())
         mid_s[...] = forward(xs[c].reshape(rows, width), w1, q1, in1, d1, q)
         os[c] = forward(mid_s[...], w2, q2, in2, d2, steps * q).reshape(n, q, width)
-        own_out(0, c).start()
-        peers(lambda peer: outbound(0, c, peer, me).start())
+        pl.when(c < AT_ONCE)(lambda: ship(0, c))
         own_in(1, c).wait()
         peers(lambda peer: inbound(1, c, peer, peer).wait_recv())
         gmid = backward(gs[c].reshape(rows, width), mid_s[...], w2, q2, in2, d2, steps * q, ac2, ap2)
         gxs[c] = backward(gmid, xs[c].reshape(rows, width), w1, q1, in1, d1, q, ac1, ap1).reshape(n, q, width)
-        own_out(1, c).start()
-        peers(lambda peer: outbound(1, c, peer, me).start())
+        pl.when(c < AT_ONCE)(lambda: ship(1, c))
         return carry
 
     lax.fori_loop(0, CHUNKS, chunk, 0)
@@ -343,6 +347,9 @@
 
             lax.fori_loop(0, count, give, 0)
             exchange(b, s).start()
+        for c in LATE.get(s, ()):
+            ship(0, c)
+            ship(1, c)
         if s:
             for b in range(2):
                 def keep(m, carry):

time: 117 us -> 108 us (0.923)
  Pallas kernels: 110 us -> 101 us
    pallas_call x1, Pallas kernels: 110 us -> 101 us  [per_device(): pl.pallas_call(functools.partial(mega, n, part, SECOND_SPACING // FIRST_S...]
where the time goes in v3:
time: 108 us
  Pallas kernels  101 us (94%)
  local copies, waits for them, and re-layouts  6.46 us (6%)
    pallas_call x1, Pallas kernels, per_device(): pl.pallas_call(functools.partial(mega, n, part, SECOND_SPACING // FIRST_S...  101 us
    unnamed x16, local copies, waits for them, and re-layouts  6.46 us

profile of v3, /device:TPU:0, one launch (start us, length us, event | category | flops | bytes accessed | tf_op | source)
XLA Modules:
  0.0 108.3 jit_solution(13347735869739138143)
XLA Ops:
  0.6 101.2 %shard_map.109 = (bf16[1024,768]{1,0:T(8,128)(2,1)}, bf16[1024,768]{1,0:T(8,128)(2,1)}, f32[72,384]{1,0:T(8,128)}, f32[24,384]{1,0:T(8,128)}, f32[72,384]{1,0:T(8,128)}, /*index=5*/f32[24,384]{1,0:T(8,128)}) custom-call(bf16[1024,768]{1,0:T(8,128)(2,1)} %tok.1, bf16[1024,768]{1,0:T(8,128)(2,1)} %cot.1, bf16[2304,384]{1,0:T(8,128)(2,1)} %c1.1, ...), custom_call_target="tpu_custom_call" | custom-call | tf_op jit(solution)/shard_map/pallas_call | solution.py:406
  101.8 0.0 copy-start
  101.8 2.8 %copy.18 = bf16[1024,768]{1,0:T(8,128)(2,1)} copy(bf16[1024,768]{1,0:T(8,128)(2,1)} %get-tuple-element.12) | data formatting | bytes 3145728
  104.6 0.0 copy-done
  104.6 0.0 copy-start.2
  104.6 0.0 copy-start.4
  104.6 0.0 copy-start.1
  104.6 0.0 copy-start.3
  104.6 1.1 %copy.19 = bf16[1024,768]{1,0:T(8,128)(2,1)} copy(bf16[1024,768]{1,0:T(8,128)(2,1)S(1)} %copy-done) | data formatting | bytes 3145728
  105.8 0.0 copy-done.2
  105.8 0.6 copy.20
  106.4 0.0 copy-done.4
  106.4 0.6 copy.21
  107.0 0.0 copy-done.1
  107.0 0.6 copy.22
  107.7 0.0 copy-done.3
  107.7 0.6 copy.23
Async XLA Ops:
  101.8 2.8 %copy-start = (bf16[1024,768]{1,0:T(8,128)(2,1)S(1)}, bf16[1024,768]{1,0:T(8,128)(2,1)}, u32[]{:S(2)}) copy-start(bf16[1024,768]{1,0:T(8,128)(2,1)} %get-tuple-element.13) | copy-start | bytes 4718596
  104.6 1.2 %copy-start.2 = (f32[72,384]{1,0:T(8,128)S(1)}, f32[72,384]{1,0:T(8,128)}, u32[]{:S(2)}) copy-start(f32[72,384]{1,0:T(8,128)} %get-tuple-element.14) | copy-start | bytes 331780
  104.6 1.8 %copy-start.4 = (f32[24,384]{1,0:T(8,128)S(1)}, f32[24,384]{1,0:T(8,128)}, u32[]{:S(2)}) copy-start(f32[24,384]{1,0:T(8,128)} %get-tuple-element.15) | copy-start | bytes 110596
  104.6 2.4 %copy-start.1 = (f32[72,384]{1,0:T(8,128)S(1)}, f32[72,384]{1,0:T(8,128)}, u32[]{:S(2)}) copy-start(f32[72,384]{1,0:T(8,128)} %get-tuple-element.16) | copy-start | bytes 331780
  104.6 3.1 %copy-start.3 = (f32[24,384]{1,0:T(8,128)S(1)}, f32[24,384]{1,0:T(8,128)}, u32[]{:S(2)}) copy-start(f32[24,384]{1,0:T(8,128)} %get-tuple-element.17) | copy-start | bytes 110596
